TPU v7x, 32 devices: a whole 2x2x4 slice. The times are simulated.
32 devices in a mesh: ctx: 8 (over y, x, core), tp: 4 (over z).
Axes of the slice: x: 2, y: 2, z: 4, core: 2. Of those that a mesh axis runs over, the one named last changes fastest.
Arguments:
- inputs: bfloat16 [4096, 2048], P(('ctx', 'tp')), may hold values from -54 to 54
- norm_gain: float32 [2048], replicated, may hold values from 0.1 to 1.9
- qkv_weight: bfloat16 [2048, 3, 2048], P(None, None, 'tp'), may hold values from -0.125 to 0.125
- head_gain: float32 [2048], P('tp'), may hold values from 0.1 to 1.9
- out_weight: bfloat16 [2048, 2048], P('tp'), may hold values from -0.125 to 0.125
- out_cotangent: bfloat16 [4096, 2048], P(('ctx', 'tp')), may hold values from -6 to 6
Outputs:
- outputs: bfloat16 [4096, 2048], P(('ctx', 'tp'))
- input_grad: bfloat16 [4096, 2048], P(('ctx', 'tp'))
- qkv_grad: float32 [2048, 3, 2048], P('ctx', None, 'tp')
- out_grad_t: float32 [2048, 2048], P('ctx', 'tp')
All inputs are finite; a program needn't handle non-finite values.
Results may differ from a plain program's by a relative error of at most 0.015.
The roundings to bfloat16 on the way count: a program that leaves them out, or rounds other values in their place, can miss the bound.
Values may be sent and summed in bfloat16 or wider, within the bound.
A program may use at most 128 MiB of HBM per device.

v0:
```python
import math
import jax
import jax.numpy as jnp
from jax import lax
from jax.sharding import PartitionSpec as P

DH = 128
EPSILON = 1e-05
highest = lax.Precision.HIGHEST


def carried_in(array, axis, combine, identity, reverse):
    devices, place = (lax.axis_size(axis), lax.axis_index(axis))
    everything = lax.all_gather(array.astype(jnp.bfloat16), axis)
    start = jnp.broadcast_to(jnp.asarray(identity, array.dtype), array.shape)

    def hop(k, before):
        at = devices - 1 - k if reverse else k
        reached = at > place if reverse else at < place
        new = combine(before, everything[at].astype(array.dtype))
        return jnp.where(reached, new, before)

    return lax.fori_loop(0, devices, hop, start)


def row_scale(rows):
    return lax.rsqrt(jnp.mean(rows * rows, axis=-1, keepdims=True) + EPSILON)


def add_states(earlier, later):
    return earlier + later


def shards(inputs, norm_gain, qkv_weight, head_gain, out_weight, out_cotangent):
    width = inputs.shape[1]
    local_width = qkv_weight.shape[2]
    heads = local_width // DH
    own_rows = inputs.shape[0]
    block = own_rows * lax.axis_size("tp")
    total_tokens = block * lax.axis_size("ctx")
    factor = 1.0 / math.sqrt(total_tokens)
    ctx_rows = width // lax.axis_size("ctx")
    flat_weight = qkv_weight.reshape(width, 3 * local_width)
    piece_f = lax.all_gather(inputs, "tp", axis=0, tiled=True).astype(jnp.float32)
    normed_rows = (piece_f * row_scale(piece_f) * norm_gain).astype(jnp.bfloat16)
    projected_rows = jnp.dot(normed_rows, flat_weight, preferred_element_type=jnp.float32).astype(
        jnp.bfloat16
    )
    joined = jnp.concatenate([normed_rows, projected_rows], axis=1)
    normed = joined[:, :width]
    projected = joined[:, width:].reshape(block, 3, heads, DH)
    queries = projected[:, 0]
    key_rows = projected[:, 1]
    values = projected[:, 2]
    local_states = jnp.einsum("shd,she->hde", key_rows, values, preferred_element_type=jnp.float32)
    empty_states = jnp.zeros_like(local_states)
    states = carried_in(local_states, "ctx", add_states, empty_states, False)
    causal = jnp.arange(block)[:, None] >= jnp.arange(block)[None, :]
    raw_scores = jnp.einsum("thd,shd->hts", queries, key_rows, preferred_element_type=jnp.float32)
    scores = jnp.where(causal[None], raw_scores, 0.0).astype(jnp.bfloat16)
    local_part = jnp.einsum("hts,she->the", scores, values, preferred_element_type=jnp.float32)
    carried = jnp.einsum("thd,hde->the", queries.astype(jnp.float32), states, precision=highest)
    attended = local_part + carried
    scale_head = row_scale(attended)
    gains = head_gain.reshape(heads, DH)
    mixed = (attended * scale_head * gains).astype(jnp.bfloat16).reshape(block, local_width)
    rows = mixed
    attn_sum = lax.psum_scatter(
        jnp.dot(rows, out_weight, preferred_element_type=jnp.float32).astype(jnp.bfloat16),
        "tp",
        scatter_dimension=0,
        tiled=True,
    ).astype(jnp.float32)
    inputs_f = inputs.astype(jnp.float32)
    outputs = (inputs_f + attn_sum).astype(jnp.bfloat16)
    cotangent = lax.all_gather(out_cotangent, "tp", axis=0, tiled=True)
    grad_mixed = lax.dot_general(
        cotangent, out_weight, (((1,), (1,)), ((), ())), preferred_element_type=jnp.float32
    ).reshape(block, heads, DH)
    weighted = grad_mixed * gains
    cube_head = scale_head * scale_head * scale_head
    grad_attended = (
        scale_head * weighted
        - cube_head * attended * jnp.mean(weighted * attended, axis=-1, keepdims=True)
    ).astype(jnp.bfloat16)
    local_grads = jnp.einsum(
        "thd,the->hde", queries, grad_attended, preferred_element_type=jnp.float32
    )
    columns = cotangent
    out_grad_t = lax.psum_scatter(
        (
            lax.dot_general(
                columns, mixed, (((0,), (0,)), ((), ())), preferred_element_type=jnp.float32
            )
            * factor
        ).astype(jnp.bfloat16),
        "ctx",
        scatter_dimension=0,
        tiled=True,
    ).astype(jnp.float32)
    raw_grad = jnp.einsum("the,she->hts", grad_attended, values, preferred_element_type=jnp.float32)
    grad_scores = jnp.where(causal[None], raw_grad, 0.0).astype(jnp.bfloat16)
    grad_query = (
        jnp.einsum("hts,shd->thd", grad_scores, key_rows, preferred_element_type=jnp.float32)
        + jnp.einsum("the,hde->thd", grad_attended.astype(jnp.float32), states, precision=highest)
    ).astype(jnp.bfloat16)
    grad_states = carried_in(local_grads, "ctx", add_states, empty_states, True)
    grad_key = jnp.einsum(
        "hts,thd->shd", grad_scores, queries, preferred_element_type=jnp.float32
    ) + jnp.einsum("she,hde->shd", values.astype(jnp.float32), grad_states, precision=highest)
    grad_value = jnp.einsum(
        "hts,the->she", scores, grad_attended, preferred_element_type=jnp.float32
    ) + jnp.einsum("shd,hde->she", key_rows.astype(jnp.float32), grad_states, precision=highest)
    grad_key, grad_value = (grad_key.astype(jnp.bfloat16), grad_value.astype(jnp.bfloat16))
    grad_proj = jnp.stack([grad_query, grad_key, grad_value], axis=1).reshape(
        block, 3 * local_width
    )
    columns = normed
    product = lax.dot_general(
        columns, grad_proj, (((0,), (0,)), ((), ())), preferred_element_type=jnp.float32
    )
    qkv_grad = lax.psum_scatter(
        (product * factor)
        .reshape(ctx_rows * lax.axis_size("ctx"), 3, local_width)
        .astype(jnp.bfloat16),
        "ctx",
        scatter_dimension=0,
        tiled=True,
    ).astype(jnp.float32)
    rows = grad_proj
    grad_normed = lax.psum_scatter(
        lax.dot_general(
            rows, flat_weight, (((1,), (1,)), ((), ())), preferred_element_type=jnp.float32
        ).astype(jnp.bfloat16),
        "tp",
        scatter_dimension=0,
        tiled=True,
    ).astype(jnp.float32)
    scale_in = row_scale(inputs_f)
    weighted_in = grad_normed * norm_gain
    cube_in = scale_in * scale_in * scale_in
    input_grad = (
        out_cotangent.astype(jnp.float32)
        + scale_in * weighted_in
        - cube_in * inputs_f * jnp.mean(weighted_in * inputs_f, axis=-1, keepdims=True)
    ).astype(jnp.bfloat16)
    return (outputs, input_grad, qkv_grad, out_grad_t)


def solution(mesh):
    in_specs = (
        P(("ctx", "tp"), None),
        P(),
        P(None, None, "tp"),
        P("tp"),
        P("tp", None),
        P(("ctx", "tp"), None),
    )
    out_specs = (
        P(("ctx", "tp"), None),
        P(("ctx", "tp"), None),
        P("ctx", None, "tp"),
        P("ctx", "tp"),
    )
    return jax.shard_map(shards, mesh=mesh, in_specs=in_specs, out_specs=out_specs, check_vma=False)
```

profile of v0, /device:TPU:0, one launch (start us, length us, event | category | flops | bytes accessed | tf_op | source)
XLA Modules:
  0.0 377.1 jit_solution(10722562484087680778)
XLA Ops:
  8.7 8.8 %copy.45 = bf16[2048,3,512]{0,2,1:T(8,128)(2,1)} copy(bf16[2048,3,512]{2,0,1:T(8,128)(2,1)} %param.12) | data formatting | bytes 12582912 | tf_op args[2]
  17.6 40.7 %all-gather.7.cloned.1.call-done = bf16[512,2048]{1,0:T(8,128)(2,1)} async-done(((bf16[128,2048]{1,0:T(8,128)(2,1)}), bf16[512,2048]{1,0:T(8,128)(2,1)}) %all-gather.7.cloned.1.call-update) | async-done | bytes 2097168 | tf_op jit(solution)/shard_map/all_gather | solution.py:44
  58.3 2.2 fusion
  60.5 7.6 %convolution_convert_fusion.2 = bf16[512,1536]{1,0:T(8,128)(2,1)} fusion(bf16[2048,1536]{0,1:T(8,128)(2,1)} %bitcast.80, bf16[512,2048]{1,0:T(8,128)(2,1)S(1)} %copy-done.12, f32[2048]{0:T(1024)S(1)} %copy-done.19, f32[512]{0:T(512)S(1)} %add_rsqrt_fusion.1), kind=kOutput, calls=%fused_computation.13 | convolution fusion | flops 3226206208 | bytes 9971712 | tf_op jit(solution)/shard_map/dot_general | solution.py:46
  68.1 3.9 %reshape.88 = bf16[512,3,4,128]{3,2,1,0:T(4,128)(2,1)} reshape(bf16[512,1536]{1,0:T(8,128)(2,1)} %convolution_convert_fusion.2) | data formatting | bytes 3145728 | tf_op jit(solution)/shard_map/reshape | solution.py:51
  72.1 2.9 fusion.26
  74.9 1.3 copy.75
  76.3 2.2 convolution_convert_fusion.4
  78.7 1.9 select_convert_fusion.1
  80.7 1.4 copy-done.1
  82.0 1.8 fusion.22
  83.8 20.7 %all-gather.9.cloned.1.call-done = bf16[512,2048]{1,0:T(8,128)(2,1)} async-done(((bf16[128,2048]{1,0:T(8,128)(2,1)}), bf16[512,2048]{1,0:T(8,128)(2,1)}) %all-gather.9.cloned.1.call-update) | async-done | bytes 2097168 | tf_op jit(solution)/shard_map/all_gather | solution.py:76
  104.5 3.8 %fusion.27 = f32[512,512]{0,1:T(8,128)} fusion(bf16[512,2048]{1,0:T(8,128)(2,1)} %all-gather.9.cloned.1.call-done, bf16[512,2048]{1,0:T(8,128)(2,1)S(1)} %copy-done), kind=kOutput, calls=%fused_computation.62 | convolution fusion | flops 1073741824 | bytes 5242880 | tf_op jit(solution)/shard_map/dot_general | solution.py:77
  108.4 20.9 %all-gather.11.cloned.1.call-done = bf16[32,128,128]{2,1,0:T(8,128)(2,1)} async-done(((bf16[4,128,128]{2,1,0:T(8,128)(2,1)}), bf16[32,128,128]{2,1,0:T(8,128)(2,1)}) %all-gather.11.cloned.1.call-update) | async-done | bytes 1048592 | tf_op jit(solution)/shard_map/all_gather | solution.py:14
  129.2 8.5 %while.30 = (s32[]{:T(128)}, f32[4,128,128]{2,1,0:T(8,128)S(1)}, s32[]{:T(128)}, bf16[8,4,128,128]{3,2,1,0:T(8,128)(2,1)}, s32[]{:T(128)}, /*index=5*/s32[]{:T(128)}) while((s32[]{:T(128)}, f32[4,128,128]{2,1,0:T(8,128)S(1)}, s32[]{:T(128)}, bf16[8,4,128,128]{3,2,1,0:T(8,128)(2,1)}, s32[]{:T(128)}, /*index=5*/s32[]{:T(128)}) %tuple.107), condition=%wide.region_2.3_spmd.clone, body=%wide.region_1.2_spmd.clone.sunk | while | flops 262148 | bytes 655461 | solution.py:23
  130.3 1.0 add_select_fusion.4
  131.3 1.0 add_select_fusion.4
  133.5 1.0 add_select_fusion.4
  134.5 1.0 add_select_fusion.4
  136.6 1.0 add_select_fusion.4
  137.7 2.4 multiply_reduce_fusion
  140.2 1.2 subtract_convert_fusion
  143.5 2.1 select_convert_fusion
  146.6 1.4 fusion.10
  148.2 1.4 fusion.28
  149.6 1.5 fusion.24
  151.8 2.6 fusion.3
  154.5 12.4 %all-gather.13.cloned.1.call-done = bf16[32,128,128]{2,1,0:T(8,128)(2,1)} async-done(((bf16[4,128,128]{2,1,0:T(8,128)(2,1)}), bf16[32,128,128]{2,1,0:T(8,128)(2,1)}) %all-gather.13.cloned.1.call-update) | async-done | bytes 1048592 | tf_op jit(solution)/shard_map/all_gather | solution.py:14
  166.8 8.6 %while.31 = (s32[]{:T(128)}, f32[4,128,128]{2,1,0:T(8,128)S(1)}, s32[]{:T(128)}, bf16[8,4,128,128]{3,2,1,0:T(8,128)(2,1)}, s32[]{:T(128)}, /*index=5*/s32[]{:T(128)}, s32[]{:T(128)}, s32[]{:T(128)}) while((s32[]{:T(128)}, f32[4,128,128]{2,1,0:T(8,128)S(1)}, s32[]{:T(128)}, bf16[8,4,128,128]{3,2,1,0:T(8,128)(2,1)}, s32[]{:T(128)}, ...), condition=%wide.region_8.9_spmd.clone, body=%wide.region_7.8_spmd.clone.sunk | while | flops 262152 | bytes 655523 | solution.py:23
  166.8 1.1 add_select_fusion.5
  168.0 1.0 add_select_fusion.5
  169.0 1.0 add_select_fusion.5
  170.1 1.0 add_select_fusion.5
  174.4 1.0 add_select_fusion.5
  175.4 2.1 fusion.8
  178.4 1.1 copy-done.14
  179.5 7.7 %convolution_convert_fusion = bf16[512,2048]{1,0:T(8,128)(2,1)} fusion(bf16[512,1536]{0,1:T(8,128)(2,1)S(1)} %bitcast.84, bf16[2048,1536]{0,1:T(8,128)(2,1)} %bitcast.81), kind=kOutput, calls=%fused_computation.11 | convolution fusion | flops 3222274048 | bytes 9961472 | tf_op jit(solution)/shard_map/dot_general | solution.py:132
  188.3 2.6 convolution_convert_fusion.1
  191.2 8.3 %multiply_convert_fusion = bf16[2048,1536]{0,1:T(8,128)(2,1)} fusion(bf16[512,1536]{0,1:T(8,128)(2,1)} %bitcast.85, bf16[512,2048]{1,0:T(8,128)(2,1)} %all-gather.7.cloned.1.call-done, f32[2048]{0:T(1024)S(1)} %copy-done.19, f32[512]{0:T(512)S(1)} %add_rsqrt_fusion.1), kind=kOutput, calls=%fused_computation.2 | convolution fusion | flops 3231711232 | bytes 9971712 | tf_op jit(solution)/shard_map/dot_general | solution.py:119
  199.4 8.7 %copy.61 = bf16[2048,3,512]{2,0,1:T(8,128)(2,1)} copy(bf16[2048,3,512]{0,2,1:T(8,128)(2,1)} %bitcast.82) | data formatting | bytes 12582912 | tf_op jit(solution)/shard_map/convert_element_type | solution.py:125
  208.1 3.1 reduce-scatter.11.cloned.1.call-done
  211.2 1.9 copy.62
  213.1 44.2 %reduce-scatter.7.cloned.1.call-done = bf16[128,2048]{1,0:T(8,128)(2,1)} async-done(((bf16[512,2048]{1,0:T(8,128)(2,1)}), bf16[128,2048]{1,0:T(8,128)(2,1)}) %reduce-scatter.7.cloned.1.call-update) | async-done | bytes 524304 | tf_op jit(solution)/shard_map/reduce_scatter | solution.py:131
  257.4 1.4 fusion.12
  258.7 44.1 %reduce-scatter.5.cloned.1.call-done = bf16[128,2048]{1,0:T(8,128)(2,1)} async-done(((bf16[512,2048]{1,0:T(8,128)(2,1)}), bf16[128,2048]{1,0:T(8,128)(2,1)}) %reduce-scatter.5.cloned.1.call-update) | async-done | bytes 524304 | tf_op jit(solution)/shard_map/reduce_scatter | solution.py:68
  302.9 2.7 fusion.15
  305.5 62.2 %reduce-scatter.9.cloned.1.call-done = bf16[256,3,512]{2,0,1:T(8,128)(2,1)} async-done(((bf16[2048,3,512]{2,0,1:T(8,128)(2,1)}), bf16[256,3,512]{2,0,1:T(8,128)(2,1)}) %reduce-scatter.9.cloned.1.call-update) | async-done | bytes 786448 | tf_op jit(solution)/shard_map/reduce_scatter | solution.py:122
  367.8 2.5 convert_element_type.139
  (75 shorter events, 14.1 us)
Async XLA Ops:
  7.2 97.3 %copy-start = (bf16[512,2048]{1,0:T(8,128)(2,1)S(1)}, bf16[512,2048]{1,0:T(8,128)(2,1)}, u32[]{:S(2)}) copy-start(bf16[512,2048]{1,0:T(8,128)(2,1)} %param.14) | copy-start | bytes 6291460
  7.2 51.1 %all-gather.7.cloned.1.call-start = ((), (), s32[]{:S(2)}) async-start(), calls=%async_computation.4 | async-start | bytes 2621440 | tf_op jit(solution)/shard_map/all_gather | solution.py:44
  7.9 96.6 %all-gather.9.cloned.1.call-start = ((), (), s32[]{:S(2)}) async-start(), calls=%async_computation.6 | async-start | bytes 2621440 | tf_op jit(solution)/shard_map/all_gather | solution.py:76
  8.7 120.6 %all-gather.11.cloned.1.call-start = ((), (), s32[]{:S(2)}) async-start(), calls=%async_computation.10 | async-start | bytes 1179648 | tf_op jit(solution)/shard_map/all_gather | solution.py:14
  8.7 51.8 %copy-start.19 = (f32[2048]{0:T(1024)S(1)}, f32[2048]{0:T(1024)}, u32[]{:S(2)}) copy-start(f32[2048]{0:T(1024)} %param.11) | copy-start | bytes 24580
  58.3 2.2 copy-start.12
  76.2 4.4 %copy-start.3 = (bf16[512,1,4,128]{0,3,2,1:T(8,128)(2,1)}, bf16[512,1,4,128]{0,3,2,1:T(8,128)(2,1)S(1)}, u32[]{:S(2)}) copy-start(bf16[512,1,4,128]{0,3,2,1:T(8,128)(2,1)S(1)} %copy.75) | copy-start | bytes 1572868
  78.5 88.3 %all-gather.13.cloned.1.call-start = ((), (), s32[]{:S(2)}) async-start(), calls=%async_computation.11 | async-start | bytes 1179648 | tf_op jit(solution)/shard_map/all_gather | solution.py:14
  78.7 2.0 copy-start.17
  80.6 1.4 copy-start.1
  108.4 29.4 %copy-start.20 = (f32[512]{0:T(512)S(1)}, f32[512]{0:T(512)}, u32[]{:S(2)}) copy-start(f32[512]{0:T(512)} %param.13) | copy-start | bytes 6148
  137.7 2.5 copy-start.10
  140.2 3.2 copy-start.18
  141.4 0.8 copy-start.6
  143.2 68.0 %reduce-scatter.11.cloned.1.call-start = ((), (), s32[]{:S(2)}) async-start(), calls=%async_computation.9 | async-start | bytes 2359296 | tf_op jit(solution)/shard_map/reduce_scatter | solution.py:90
  143.4 2.1 copy-start.5
  145.6 1.0 copy-start.7
  146.6 1.6 copy-start.2
  149.6 1.5 copy-start.15
  149.6 2.2 copy-start.21
  154.4 102.9 %reduce-scatter.7.cloned.1.call-start = ((), (), s32[]{:S(2)}) async-start(), calls=%async_computation.7 | async-start | bytes 2621440 | tf_op jit(solution)/shard_map/reduce_scatter | solution.py:131
  166.8 10.7 %copy-start.4 = (bf16[512,1,4,128]{0,3,2,1:T(8,128)(2,1)S(1)}, bf16[512,1,4,128]{0,3,2,1:T(8,128)(2,1)}, u32[]{:S(2)}) copy-start(bf16[512,1,4,128]{0,3,2,1:T(8,128)(2,1)} %copy-done.3) | copy-start | bytes 1572868
  175.4 2.2 copy-start.9
  175.4 2.8 copy-start.13
  178.4 1.1 copy-start.14
  187.2 1.0 copy-start.16
  187.3 115.6 %reduce-scatter.5.cloned.1.call-start = ((), (), s32[]{:S(2)}) async-start(), calls=%async_computation.5 | async-start | bytes 2621440 | tf_op jit(solution)/shard_map/reduce_scatter | solution.py:68
  190.9 176.9 %reduce-scatter.9.cloned.1.call-start = ((), (), s32[]{:S(2)}) async-start(), calls=%async_computation.8 | async-start | bytes 7077888 | tf_op jit(solution)/shard_map/reduce_scatter | solution.py:122
  208.1 49.3 %copy-start.8 = (bf16[128,2048]{1,0:T(8,128)(2,1)S(1)}, bf16[128,2048]{1,0:T(8,128)(2,1)}, u32[]{:S(2)}) copy-start(bf16[128,2048]{1,0:T(8,128)(2,1)} %param.10) | copy-start | bytes 1572868
  208.1 94.8 %copy-start.11 = (bf16[128,2048]{1,0:T(8,128)(2,1)S(1)}, bf16[128,2048]{1,0:T(8,128)(2,1)}, u32[]{:S(2)}) copy-start(bf16[128,2048]{1,0:T(8,128)(2,1)} %param.15) | copy-start | bytes 1572868
Sparse Core Ops, SparseCore 0:
  9.6 48.6 all-gather.6
  59.8 44.6 all-gather.8
  107.0 22.1 all-gather.10
  143.3 23.4 all-gather.12
  170.0 41.2 reduce-scatter.10
  213.5 43.8 reduce-scatter.6
  259.6 43.1 reduce-scatter.4
  306.6 61.1 reduce-scatter.8
where the time goes:
time: 379 us; the launch traced here: 377 us
  waiting for transfers between devices  250 us (66%)
  matrix products  52 us (14%)
  local copies, waits for them, and re-layouts  33 us (9%)
  other arithmetic  26.8 us (7%)
  between operations  14.5 us (4%)
    reduce_scatter x1, waiting for transfers between devices, shards(): lax.psum_scatter((product * factor).reshape(ctx_rows * lax.axis_size('ctx...  62.2 us
    reduce_scatter x1, waiting for transfers between devices, shards(): lax.psum_scatter(lax.dot_general(rows, flat_weight, (((1,), (1,)), ((), (...  44.2 us
    reduce_scatter x1, waiting for transfers between devices, shards(): lax.psum_scatter(jnp.dot(rows, out_weight, preferred_element_type=jnp.flo...  44.1 us
    all_gather x1, waiting for transfers between devices, shards(): lax.all_gather(inputs, 'tp', axis=0, tiled=True).astype(jnp.float32)  40.7 us
    all_gather x2, waiting for transfers between devices, carried_in(): everything = lax.all_gather(array.astype(jnp.bfloat16), axis)  33.2 us
    all_gather x1, waiting for transfers between devices, shards(): cotangent = lax.all_gather(out_cotangent, 'tp', axis=0, tiled=True)  20.7 us
    unnamed x47, local copies, waits for them, and re-layouts  17.5 us
    select_n x16, other arithmetic, hop(): return jnp.where(reached, new, before)  16.7 us
  transfers between devices with their start and end apart: 8, of which 8 were waited for; matrix products, arithmetic and copies ran while one was open for 24% of the time, Pallas kernels for 0%

commit v1 on v0

--- a/solution.py
+++ b/solution.py
@@ -73,7 +73,30 @@
     ).astype(jnp.float32)
     inputs_f = inputs.astype(jnp.float32)
     outputs = (inputs_f + attn_sum).astype(jnp.bfloat16)
-    cotangent = lax.all_gather(out_cotangent, "tp", axis=0, tiled=True)
+    z = lax.axis_size("tp")
+    local_next = lax.axis_index("tp")
+    lower, parts_out, plain = (z, local_next, out_cotangent.shape[0])
+    pieces_in = [dd * lower if pp == 0 else dd for pp, dd in enumerate(out_cotangent.shape)]
+    cotangent = lax.dynamic_update_slice_in_dim(
+        jnp.zeros(pieces_in, out_cotangent.dtype), out_cotangent, parts_out * plain, axis=0
+    )
+    clean = p_next = out_cotangent
+    hop_no = 1
+    while hop_no < lower // 2 + 1:
+        clean = lax.ppermute(
+            clean, axis_name="tp", perm=[(pp, (pp + 1) % lower) for pp in range(lower)]
+        )
+        cotangent = lax.dynamic_update_slice_in_dim(
+            cotangent, clean, (parts_out - hop_no) % lower * plain, axis=0
+        )
+        if 2 * hop_no < lower:
+            p_next = lax.ppermute(
+                p_next, axis_name="tp", perm=[(pp, (pp - 1) % lower) for pp in range(lower)]
+            )
+            cotangent = lax.dynamic_update_slice_in_dim(
+                cotangent, p_next, (parts_out + hop_no) % lower * plain, axis=0
+            )
+        hop_no = hop_no + 1
     grad_mixed = lax.dot_general(
         cotangent, out_weight, (((1,), (1,)), ((), ())), preferred_element_type=jnp.float32
     ).reshape(block, heads, DH)

time: 379 us -> 374 us (0.987)
  waiting for transfers between devices: 250 us -> 226 us
  starting transfers between devices: 0.72 us -> 11.5 us
  local copies, waits for them, and re-layouts: 33 us -> 37.9 us
    all_gather x1 -> x0, waiting for transfers between devices: 20.7 us -> none  [shards(): cotangent = lax.all_gather(out_cotangent, 'tp', axis=0, tiled=True)]
    all_gather x2, waiting for transfers between devices: 33.2 us -> 19.8 us  [carried_in(): everything = lax.all_gather(array.astype(jnp.bfloat16), axis)]
    ppermute x0 -> x3, starting transfers between devices: none -> 10.8 us  [the longest x2 8.68 us: shards(): lax.ppermute(clean, axis_name='tp', perm=[(pp, (pp + 1) % lower) for pp i...]
    all_gather x1, waiting for transfers between devices: 40.7 us -> 48.6 us  [shards(): lax.all_gather(inputs, 'tp', axis=0, tiled=True).astype(jnp.float32)]
    dynamic_update_slice x0 -> x4, local copies, waits for them, and re-layouts: none -> 6.57 us  [the longest x2 3.79 us: shards(): lax.dynamic_update_slice_in_dim(cotangent, clean, (parts_out - hop_no) %...]
    unnamed x47 -> x48, local copies, waits for them, and re-layouts: 17.5 us -> 14.2 us
  transfers between devices with their start and end apart: 8 -> 10, of which waited for: 8 -> 8; matrix products, arithmetic and copies ran while one was open for 24% -> 27% of each run, Pallas kernels for 0% -> 0%
where the time goes in v1:
time: 374 us; the launch traced here: 372 us
  waiting for transfers between devices  226 us (60%)
  matrix products  52.5 us (14%)
  local copies, waits for them, and re-layouts  37.9 us (10%)
  other arithmetic  29.4 us (8%)
  between operations  14.4 us (4%)
  starting transfers between devices  11.5 us (3%)
    reduce_scatter x1, waiting for transfers between devices, shards(): lax.psum_scatter((product * factor).reshape(ctx_rows * lax.axis_size('ctx...  62.2 us
    all_gather x1, waiting for transfers between devices, shards(): lax.all_gather(inputs, 'tp', axis=0, tiled=True).astype(jnp.float32)  48.6 us
    reduce_scatter x1, waiting for transfers between devices, shards(): lax.psum_scatter(lax.dot_general(rows, flat_weight, (((1,), (1,)), ((), (...  44.3 us
    reduce_scatter x1, waiting for transfers between devices, shards(): lax.psum_scatter(jnp.dot(rows, out_weight, preferred_element_type=jnp.flo...  44 us
    all_gather x2, waiting for transfers between devices, carried_in(): everything = lax.all_gather(array.astype(jnp.bfloat16), axis)  19.8 us
    select_n x16, other arithmetic, hop(): return jnp.where(reached, new, before)  16.7 us
    unnamed x48, local copies, waits for them, and re-layouts  14.2 us
    ppermute x2, starting transfers between devices, shards(): lax.ppermute(clean, axis_name='tp', perm=[(pp, (pp + 1) % lower) for pp i...  8.68 us
  transfers between devices with their start and end apart: 10, of which 8 were waited for; matrix products, arithmetic and copies ran while one was open for 27% of the time, Pallas kernels for 0%

profile of v1, /device:TPU:0, one launch (start us, length us, event | category | flops | bytes accessed | tf_op | source)
XLA Modules:
  0.0 372.0 jit_solution(8122877512697547511)
XLA Ops:
  8.0 3.1 collective-permute-start
  11.0 2.1 collective-permute-start.1
  13.1 9.0 %copy.43 = bf16[2048,3,512]{0,2,1:T(8,128)(2,1)} copy(bf16[2048,3,512]{2,0,1:T(8,128)(2,1)} %param.12) | data formatting | bytes 12582912 | tf_op args[2]
  22.1 1.6 broadcast_in_dim.38
  24.6 2.9 collective-permute-done
  27.6 5.6 %collective-permute-start.2 = (bf16[128,2048]{1,0:T(8,128)(2,1)}, bf16[128,2048]{1,0:T(8,128)(2,1)}, u32[]{:S(2)}, u32[]{:S(2)}) collective-permute-start(bf16[128,2048]{1,0:T(8,128)(2,1)} %collective-permute-done), channel_id=1, source_target_pairs={{0,1},{1,2},{2,3},{3,0},{4,5},{5,6},{6,7},{7,4},{8,9},{9,10},{10,1... | collective-permute-start | bytes 1572872 | tf_op jit(solution)/shard_map/ppermute | solution.py:86
  33.2 48.6 %all-gather.6.cloned.1.call-done = bf16[512,2048]{1,0:T(8,128)(2,1)} async-done(((bf16[128,2048]{1,0:T(8,128)(2,1)}), bf16[512,2048]{1,0:T(8,128)(2,1)}) %all-gather.6.cloned.1.call-update) | async-done | bytes 2097168 | tf_op jit(solution)/shard_map/all_gather | solution.py:44
  81.8 2.2 fusion
  84.1 7.6 %convolution_convert_fusion.2 = bf16[512,1536]{1,0:T(8,128)(2,1)} fusion(bf16[2048,1536]{0,1:T(8,128)(2,1)} %bitcast.78, bf16[512,2048]{1,0:T(8,128)(2,1)S(1)} %copy-done.13, f32[2048]{0:T(1024)S(1)} %copy-done.21, f32[512]{0:T(512)S(1)} %add_rsqrt_fusion.1), kind=kOutput, calls=%fused_computation.13 | convolution fusion | flops 3226206208 | bytes 9971712 | tf_op jit(solution)/shard_map/dot_general | solution.py:46
  91.7 3.9 %reshape.88 = bf16[512,3,4,128]{3,2,1,0:T(4,128)(2,1)} reshape(bf16[512,1536]{1,0:T(8,128)(2,1)} %convolution_convert_fusion.2) | data formatting | bytes 3145728 | tf_op jit(solution)/shard_map/reshape | solution.py:51
  95.6 2.9 fusion.25
  98.5 1.3 copy.72
  99.8 2.2 convolution_convert_fusion.4
  102.9 1.9 constant_dynamic-update-slice_fusion.2
  104.8 1.9 constant_dynamic-update-slice_fusion.1
  106.7 1.9 constant_dynamic-update-slice_fusion
  108.6 4.0 %fusion.26 = f32[512,512]{0,1:T(8,128)} fusion(bf16[512,2048]{1,0:T(8,128)(2,1)} %constant_dynamic-update-slice_fusion, bf16[512,2048]{1,0:T(8,128)(2,1)S(1)} %copy-done), kind=kOutput, calls=%fused_computation.65 | convolution fusion | flops 1073741824 | bytes 5242880 | tf_op jit(solution)/shard_map/dot_general | solution.py:100
  113.4 1.4 copy-done.1
  114.8 1.8 fusion.21
  116.6 8.5 %all-gather.8.cloned.1.call-done = bf16[32,128,128]{2,1,0:T(8,128)(2,1)} async-done(((bf16[4,128,128]{2,1,0:T(8,128)(2,1)}), bf16[32,128,128]{2,1,0:T(8,128)(2,1)}) %all-gather.8.cloned.1.call-update) | async-done | bytes 1048592 | tf_op jit(solution)/shard_map/all_gather | solution.py:14
  125.1 8.5 %while.30 = (s32[]{:T(128)}, f32[4,128,128]{2,1,0:T(8,128)S(1)}, s32[]{:T(128)}, bf16[8,4,128,128]{3,2,1,0:T(8,128)(2,1)}, s32[]{:T(128)}, /*index=5*/s32[]{:T(128)}) while((s32[]{:T(128)}, f32[4,128,128]{2,1,0:T(8,128)S(1)}, s32[]{:T(128)}, bf16[8,4,128,128]{3,2,1,0:T(8,128)(2,1)}, s32[]{:T(128)}, /*index=5*/s32[]{:T(128)}) %tuple.101), condition=%wide.region_2.3_spmd.clone, body=%wide.region_1.2_spmd.clone.sunk | while | flops 262148 | bytes 655461 | solution.py:23
  126.1 1.0 add_select_fusion.4
  127.2 1.0 add_select_fusion.4
  133.6 2.4 multiply_reduce_fusion
  136.0 1.2 subtract_convert_fusion
  138.5 2.1 select_convert_fusion
  141.7 1.4 fusion.9
  143.3 1.4 fusion.27
  144.7 1.5 fusion.23
  146.2 4.2 %multiply_convert_fusion.1 = bf16[2048,512]{1,0:T(8,128)(2,1)} fusion(bf16[512,2048]{1,0:T(8,128)(2,1)} %constant_dynamic-update-slice_fusion, bf16[512,512]{0,1:T(8,128)(2,1)S(1)} %bitcast.84), kind=kOutput, calls=%fused_computation.8 | convolution fusion | flops 1075838976 | bytes 4718592 | tf_op jit(solution)/shard_map/dot_general | solution.py:115
  150.5 11.4 %all-gather.10.cloned.1.call-done = bf16[32,128,128]{2,1,0:T(8,128)(2,1)} async-done(((bf16[4,128,128]{2,1,0:T(8,128)(2,1)}), bf16[32,128,128]{2,1,0:T(8,128)(2,1)}) %all-gather.10.cloned.1.call-update) | async-done | bytes 1048592 | tf_op jit(solution)/shard_map/all_gather | solution.py:14
  161.9 8.6 %while.31 = (s32[]{:T(128)}, f32[4,128,128]{2,1,0:T(8,128)S(1)}, s32[]{:T(128)}, bf16[8,4,128,128]{3,2,1,0:T(8,128)(2,1)}, s32[]{:T(128)}, /*index=5*/s32[]{:T(128)}, s32[]{:T(128)}, s32[]{:T(128)}) while((s32[]{:T(128)}, f32[4,128,128]{2,1,0:T(8,128)S(1)}, s32[]{:T(128)}, bf16[8,4,128,128]{3,2,1,0:T(8,128)(2,1)}, s32[]{:T(128)}, ...), condition=%wide.region_8.9_spmd.clone, body=%wide.region_7.8_spmd.clone.sunk | while | flops 262152 | bytes 655523 | solution.py:23
  161.9 1.1 add_select_fusion.5
  169.4 1.0 add_select_fusion.5
  170.5 2.0 fusion.7
  173.3 1.1 copy-done.17
  174.4 7.7 %convolution_convert_fusion = bf16[512,2048]{1,0:T(8,128)(2,1)} fusion(bf16[512,1536]{0,1:T(8,128)(2,1)S(1)} %bitcast.82, bf16[2048,1536]{0,1:T(8,128)(2,1)} %bitcast.79), kind=kOutput, calls=%fused_computation.11 | convolution fusion | flops 3222274048 | bytes 9961472 | tf_op jit(solution)/shard_map/dot_general | solution.py:155
  183.2 2.6 convolution_convert_fusion.1
  186.0 8.3 %multiply_convert_fusion = bf16[2048,1536]{0,1:T(8,128)(2,1)} fusion(bf16[512,1536]{0,1:T(8,128)(2,1)} %bitcast.83, bf16[512,2048]{1,0:T(8,128)(2,1)} %all-gather.6.cloned.1.call-done, f32[2048]{0:T(1024)S(1)} %copy-done.21, f32[512]{0:T(512)S(1)} %add_rsqrt_fusion.1), kind=kOutput, calls=%fused_computation.2 | convolution fusion | flops 3231711232 | bytes 9971712 | tf_op jit(solution)/shard_map/dot_general | solution.py:142
  194.3 8.6 %copy.59 = bf16[2048,3,512]{2,0,1:T(8,128)(2,1)} copy(bf16[2048,3,512]{0,2,1:T(8,128)(2,1)} %bitcast.80) | data formatting | bytes 12582912 | tf_op jit(solution)/shard_map/convert_element_type | solution.py:148
  203.0 3.3 reduce-scatter.11.cloned.1.call-done
  206.3 1.8 convert_element_type.138
  208.1 44.3 %reduce-scatter.7.cloned.1.call-done = bf16[128,2048]{1,0:T(8,128)(2,1)} async-done(((bf16[512,2048]{1,0:T(8,128)(2,1)}), bf16[128,2048]{1,0:T(8,128)(2,1)}) %reduce-scatter.7.cloned.1.call-update) | async-done | bytes 524304 | tf_op jit(solution)/shard_map/reduce_scatter | solution.py:154
  252.4 1.4 fusion.11
  253.8 44.0 %reduce-scatter.5.cloned.1.call-done = bf16[128,2048]{1,0:T(8,128)(2,1)} async-done(((bf16[512,2048]{1,0:T(8,128)(2,1)}), bf16[128,2048]{1,0:T(8,128)(2,1)}) %reduce-scatter.5.cloned.1.call-update) | async-done | bytes 524304 | tf_op jit(solution)/shard_map/reduce_scatter | solution.py:68
  297.8 2.7 fusion.14
  300.4 62.2 %reduce-scatter.9.cloned.1.call-done = bf16[256,3,512]{2,0,1:T(8,128)(2,1)} async-done(((bf16[2048,3,512]{2,0,1:T(8,128)(2,1)}), bf16[256,3,512]{2,0,1:T(8,128)(2,1)}) %reduce-scatter.9.cloned.1.call-update) | async-done | bytes 786448 | tf_op jit(solution)/shard_map/reduce_scatter | solution.py:145
  362.7 2.5 convert_element_type.136
  (85 shorter events, 20.5 us)
Async XLA Ops:
  7.2 101.4 %copy-start = (bf16[512,2048]{1,0:T(8,128)(2,1)S(1)}, bf16[512,2048]{1,0:T(8,128)(2,1)}, u32[]{:S(2)}) copy-start(bf16[512,2048]{1,0:T(8,128)(2,1)} %param.14) | copy-start | bytes 6291460
  7.2 74.6 %all-gather.6.cloned.1.call-start = ((), (), s32[]{:S(2)}) async-start(), calls=%async_computation.4 | async-start | bytes 2621440 | tf_op jit(solution)/shard_map/all_gather | solution.py:44
  7.9 117.2 %all-gather.8.cloned.1.call-start = ((), (), s32[]{:S(2)}) async-start(), calls=%async_computation.9 | async-start | bytes 1179648 | tf_op jit(solution)/shard_map/all_gather | solution.py:14
  8.0 19.6 %collective-permute-start = (bf16[128,2048]{1,0:T(8,128)(2,1)}, bf16[128,2048]{1,0:T(8,128)(2,1)}, u32[]{:S(2)}, u32[]{:S(2)}) collective-permute-start(bf16[128,2048]{1,0:T(8,128)(2,1)} %param.15), channel_id=1, source_target_pairs={{0,1},{1,2},{2,3},{3,0},{4,5},{5,6},{6,7},{7,4},{8,9},{9,10},{10,1... | collective-permute-start | bytes 1572872 | tf_op jit(solution)/shard_map/ppermute | solution.py:86
  11.0 93.8 %collective-permute-start.1 = (bf16[128,2048]{1,0:T(8,128)(2,1)}, bf16[128,2048]{1,0:T(8,128)(2,1)}, u32[]{:S(2)}, u32[]{:S(2)}) collective-permute-start(bf16[128,2048]{1,0:T(8,128)(2,1)} %param.15), channel_id=1, source_target_pairs={{0,3},{1,0},{2,1},{3,2},{4,7},{5,4},{6,5},{7,6},{8,11},{9,8},{10,9... | collective-permute-start | bytes 1572872 | tf_op jit(solution)/shard_map/ppermute | solution.py:93
  22.1 1.6 copy-start.14
  23.7 60.3 %copy-start.21 = (f32[2048]{0:T(1024)S(1)}, f32[2048]{0:T(1024)}, u32[]{:S(2)}) copy-start(f32[2048]{0:T(1024)} %param.11) | copy-start | bytes 24580
  27.6 79.2 %collective-permute-start.2 = (bf16[128,2048]{1,0:T(8,128)(2,1)}, bf16[128,2048]{1,0:T(8,128)(2,1)}, u32[]{:S(2)}, u32[]{:S(2)}) collective-permute-start(bf16[128,2048]{1,0:T(8,128)(2,1)} %collective-permute-done), channel_id=1, source_target_pairs={{0,1},{1,2},{2,3},{3,0},{4,5},{5,6},{6,7},{7,4},{8,9},{9,10},{10,1... | collective-permute-start | bytes 1572872 | tf_op jit(solution)/shard_map/ppermute | solution.py:86
  81.8 2.2 copy-start.13
  99.8 13.6 %copy-start.3 = (bf16[512,1,4,128]{0,3,2,1:T(8,128)(2,1)}, bf16[512,1,4,128]{0,3,2,1:T(8,128)(2,1)S(1)}, u32[]{:S(2)}) copy-start(bf16[512,1,4,128]{0,3,2,1:T(8,128)(2,1)S(1)} %copy.72) | copy-start | bytes 1572868
  102.1 59.8 %all-gather.10.cloned.1.call-start = ((), (), s32[]{:S(2)}) async-start(), calls=%async_computation.10 | async-start | bytes 1179648 | tf_op jit(solution)/shard_map/all_gather | solution.py:14
  108.6 4.0 %copy-start.5 = (bf16[512,1,4,128]{3,2,1,0:T(4,128)(2,1)S(1)}, bf16[512,1,4,128]{3,2,1,0:T(4,128)(2,1)}, u32[]{:S(2)}) copy-start(bf16[512,1,4,128]{3,2,1,0:T(4,128)(2,1)} %get-tuple-element.246) | copy-start | bytes 1572868
  108.6 4.0 %copy-start.20 = (pred[512,512]{1,0:T(8,128)(4,1)S(1)}, pred[512,512]{1,0:T(8,128)(4,1)}, u32[]{:S(2)}) copy-start(pred[512,512]{1,0:T(8,128)(4,1)} %iota_compare_fusion) | copy-start | bytes 786436
  113.4 1.4 copy-start.1
  116.6 17.0 %copy-start.22 = (f32[512]{0:T(512)S(1)}, f32[512]{0:T(512)}, u32[]{:S(2)}) copy-start(f32[512]{0:T(512)} %param.13) | copy-start | bytes 6148
  133.5 2.5 copy-start.12
  137.2 1.3 copy-start.8
  138.2 68.0 %reduce-scatter.11.cloned.1.call-start = ((), (), s32[]{:S(2)}) async-start(), calls=%async_computation.8 | async-start | bytes 2359296 | tf_op jit(solution)/shard_map/reduce_scatter | solution.py:113
  138.5 2.2 copy-start.6
  140.7 1.0 copy-start.9
  141.7 1.6 copy-start.2
  144.7 1.5 copy-start.18
  150.5 20.0 %copy-start.7 = (bf16[512,1,4,128]{3,2,1,0:T(4,128)(2,1)S(1)}, bf16[512,1,4,128]{3,2,1,0:T(4,128)(2,1)}, u32[]{:S(2)}) copy-start(bf16[512,1,4,128]{3,2,1,0:T(4,128)(2,1)} %get-tuple-element.246) | copy-start | bytes 1572868
  150.5 101.9 %reduce-scatter.7.cloned.1.call-start = ((), (), s32[]{:S(2)}) async-start(), calls=%async_computation.6 | async-start | bytes 2621440 | tf_op jit(solution)/shard_map/reduce_scatter | solution.py:154
  161.9 10.6 %copy-start.4 = (bf16[512,1,4,128]{0,3,2,1:T(8,128)(2,1)S(1)}, bf16[512,1,4,128]{0,3,2,1:T(8,128)(2,1)}, u32[]{:S(2)}) copy-start(bf16[512,1,4,128]{0,3,2,1:T(8,128)(2,1)} %copy-done.3) | copy-start | bytes 1572868
  170.5 2.0 copy-start.11
  170.5 2.6 copy-start.16
  173.3 1.1 copy-start.17
  182.1 1.0 copy-start.19
  182.2 115.6 %reduce-scatter.5.cloned.1.call-start = ((), (), s32[]{:S(2)}) async-start(), calls=%async_computation.5 | async-start | bytes 2621440 | tf_op jit(solution)/shard_map/reduce_scatter | solution.py:68
  185.8 176.9 %reduce-scatter.9.cloned.1.call-start = ((), (), s32[]{:S(2)}) async-start(), calls=%async_computation.7 | async-start | bytes 7077888 | tf_op jit(solution)/shard_map/reduce_scatter | solution.py:145
  203.0 49.4 %copy-start.10 = (bf16[128,2048]{1,0:T(8,128)(2,1)S(1)}, bf16[128,2048]{1,0:T(8,128)(2,1)}, u32[]{:S(2)}) copy-start(bf16[128,2048]{1,0:T(8,128)(2,1)} %param.10) | copy-start | bytes 1572868
  203.0 94.8 %copy-start.15 = (bf16[128,2048]{1,0:T(8,128)(2,1)S(1)}, bf16[128,2048]{1,0:T(8,128)(2,1)}, u32[]{:S(2)}) copy-start(bf16[128,2048]{1,0:T(8,128)(2,1)} %param.15) | copy-start | bytes 1572868
Sparse Core Ops, SparseCore 0:
  9.6 72.1 all-gather.5
  102.2 22.8 all-gather.7
  138.4 23.4 all-gather.9
  165.0 41.1 reduce-scatter.10
  208.5 43.8 reduce-scatter.6
  254.5 43.1 reduce-scatter.4
  301.5 61.1 reduce-scatter.8
